TPU v7x, 32 devices: a whole 2x2x4 slice. The times are simulated.
32 devices in a mesh: replica: 8 (over y, x, core), tok: 4 (over z).
Axes of the slice: x: 2, y: 2, z: 4, core: 2. Of those that a mesh axis runs over, the one named last changes fastest.
Arguments:
- activations: bfloat16 [8192, 2880], P(('replica', 'tok')), may hold values from -6 to 6
- cotangent: bfloat16 [8192, 512], P(('replica', 'tok')), may hold values from -6 to 6
- next_inputs: bfloat16 [8192, 2880], P(('replica', 'tok')), may hold values from -6 to 6
- weight_tiles: bfloat16 [360, 4096], P('tok'), may hold values from -0.109375 to 0.109375
- momentum: float32 [8, 360, 4096], P('replica', 'tok'), may hold values from -6 to 6
- chosen: int32 [8, 4, 8], P('replica', 'tok'), may hold values from 0 to 89, as said below
- counts: int32 [8, 4], P('replica', 'tok'), may hold values from 1 to 8, as said below
Outputs:
- values: bfloat16 [8192, 512], P(('replica', 'tok'))
- new_momentum: float32 [8, 360, 4096], P('replica', 'tok')
Inputs may be any that keep to these rules, and one draw needn't show every extreme that they name: Each list chosen[r, k] names 8 different tile numbers of the shard's 90 tiles; only the first counts[r, k] of them are selected. `counts`: in every draw some token shard has 8 selected tiles in every replica.
All inputs are finite; a program needn't handle non-finite values.
Results may differ from a plain program's by a relative error of at most 0.015.
Values may be sent and summed in bfloat16 or wider, within the bound.
No kernel may reach another device: no remote copies, remote signals or barrier semaphores. Data moves between devices by JAX's collectives and lax.ppermute only.
A program may use at most 64 MiB of HBM per device.

v0:
```python
import math
import jax
import jax.numpy as jnp
from jax import lax
from jax.sharding import PartitionSpec as P

TILE = 64
KEEP = 32
momentum_decay = 0.9
step_size = 0.01


def cosine_rows(count):
    frequency = jnp.arange(count, dtype=jnp.float32)[:, None]
    position = jnp.arange(TILE, dtype=jnp.float32)[None, :]
    cosines = jnp.cos(math.pi * (2.0 * position + 1.0) * frequency / (2.0 * TILE))
    factor = jnp.where(frequency == 0, math.sqrt(1.0 / TILE), math.sqrt(2.0 / TILE))
    return cosines * factor


def rebuild(summed, weight_part, keep_rows):
    quads = summed.reshape(summed.shape[0], KEEP, KEEP)
    update = jnp.einsum(
        "ua,tuv,vb->tab", keep_rows, quads, keep_rows, precision=lax.Precision.HIGHEST
    )
    shifted = weight_part.astype(jnp.float32) - step_size * update.reshape(
        summed.shape[0], TILE * TILE
    )
    return shifted.astype(jnp.bfloat16)


def forward(inputs, new_tiles):
    row_tiles = inputs.shape[1] // TILE
    col_tiles = new_tiles.shape[0] // row_tiles
    blocks = inputs.reshape(inputs.shape[0], row_tiles, TILE)
    matrix = new_tiles.reshape(row_tiles, col_tiles, TILE, TILE)
    output = jnp.einsum("tra,rcab->tcb", blocks, matrix, preferred_element_type=jnp.float32)
    return output.reshape(inputs.shape[0], col_tiles * TILE).astype(jnp.bfloat16)


def local(activations, cotangent, next_inputs, weight_tiles, momentum, chosen, counts):
    highest = lax.Precision.HIGHEST
    shards = lax.axis_size("tok")
    tiles_here = weight_tiles.shape[0]
    row_tiles = activations.shape[1] // TILE
    col_tiles = cotangent.shape[1] // TILE
    grad_scale = 1.0 / math.sqrt(activations.shape[0] * shards)
    keep_rows = cosine_rows(KEEP)
    row_span = min(tiles_here * lax.axis_size("tok") // col_tiles + 2, row_tiles)
    product = (
        lax.dot_general(
            activations, cotangent, (((0,), (0,)), ((), ())), preferred_element_type=jnp.float32
        )
        * grad_scale
    )
    tiled = product.reshape(row_span, TILE, col_tiles, TILE).transpose(0, 2, 1, 3)
    tiled = tiled.reshape(row_span * col_tiles, TILE * TILE)
    gradient = lax.psum_scatter(
        tiled.astype(jnp.bfloat16), "tok", scatter_dimension=0, tiled=True
    ).astype(jnp.float32)
    updated = momentum_decay * momentum[0] + gradient
    chosen_here = chosen[0, 0]
    in_list = jnp.arange(chosen_here.shape[0], dtype=jnp.int32) < counts[0, 0]
    picked = jnp.take(updated, chosen_here, axis=0).reshape(-1, TILE, TILE)
    quadrant = jnp.einsum("ua,nab,vb->nuv", keep_rows, picked, keep_rows, precision=highest)
    quadrant = jnp.where(in_list[:, None, None], quadrant, 0.0).astype(jnp.bfloat16)
    rebuilt = jnp.einsum(
        "ua,nuv,vb->nab", keep_rows, quadrant.astype(jnp.float32), keep_rows, precision=highest
    )
    new_momentum = updated.at[chosen_here].add(-rebuilt.reshape(-1, TILE * TILE))
    listed = jnp.where(in_list, chosen_here, -1)
    flat_quads = quadrant.reshape(-1, KEEP * KEEP)
    tile_numbers = jnp.arange(tiles_here, dtype=jnp.int32)
    all_quads, all_listed = (
        lax.all_gather(flat_quads, "replica", axis=0, tiled=True),
        lax.all_gather(listed, "replica", axis=0, tiled=True),
    )
    one_hot = (all_listed[:, None] == tile_numbers[None, :]).astype(jnp.bfloat16)
    summed = lax.dot_general(
        one_hot, all_quads, (((0,), (0,)), ((), ())), preferred_element_type=jnp.float32
    )
    new_part = rebuild(summed, weight_tiles, keep_rows)
    new_full = lax.all_gather(new_part, "tok", axis=0, tiled=True)
    values = forward(next_inputs, new_full)
    return (values, new_momentum[None])


def solution(mesh):
    return jax.shard_map(
        local,
        mesh=mesh,
        in_specs=(
            P(("replica", "tok"), None),
            P(("replica", "tok"), None),
            P(("replica", "tok"), None),
            P("tok", None),
            P("replica", "tok", None),
            P("replica", "tok", None),
            P("replica", "tok"),
        ),
        out_specs=(P(("replica", "tok"), None), P("replica", "tok", None)),
        check_vma=False,
    )
```

profile of v0, /device:TPU:0, one launch (start us, length us, event | category | flops | bytes accessed | tf_op | source)
XLA Modules:
  0.0 222.4 jit_solution(13789088672530609271)
XLA Ops:
  7.2 0.0 copy-start
  7.2 0.0 all-gather.3.cloned.1.call-start
  7.2 1.3 copy-done
  8.5 3.5 %multiply_convert_fusion = bf16[2880,512]{1,0:T(8,128)(2,1)} fusion(bf16[256,2880]{0,1:T(8,128)(2,1)S(1)} %copy-done, bf16[256,512]{1,0:T(8,128)(2,1)} %param.8), kind=kOutput, calls=%fused_computation.2 | convolution fusion | flops 757923840 | bytes 4685824 | tf_op jit(solution)/shard_map/dot_general | solution.py:51
  12.1 8.4 %convert_element_type.37 = bf16[45,64,8,64]{3,2,1,0:T(8,128)(2,1)} reshape(bf16[2880,512]{1,0:T(8,128)(2,1)} %multiply_convert_fusion) | data formatting | bytes 5898240 | tf_op jit(solution)/shard_map/convert_element_type | solution.py:59
  20.5 7.0 %copy.22 = bf16[45,8,64,64]{3,2,1,0:T(8,128)(2,1)} copy(bf16[45,8,64,64]{3,1,2,0:T(8,128)(2,1)} %bitcast.59) | data formatting | bytes 5898240 | tf_op jit(solution)/shard_map/convert_element_type | solution.py:59
  27.5 8.7 %convert_element_type.39 = bf16[360,4096]{1,0:T(8,128)(2,1)} reshape(bf16[45,8,64,64]{3,2,1,0:T(8,128)(2,1)} %copy.22) | data formatting | bytes 5898240 | tf_op jit(solution)/shard_map/convert_element_type | solution.py:59
  36.2 0.0 copy-start.3
  36.2 0.0 copy-start.4
  36.2 0.0 copy-start.2
  36.2 61.9 %fusion = bf16[96,4096]{1,0:T(8,128)(2,1)S(1)} fusion(bf16[360,4096]{1,0:T(8,128)(2,1)} %convert_element_type.39), kind=kCustom, calls=%all-reduce-scatter | all-reduce-scatter fusion | flops 1572865 | bytes 3736064
  98.2 1.7 collective-permute-start
  99.9 0.0 copy-done.3
  100.6 0.0 copy-done.4
  100.6 0.6 dynamic-slice
  101.9 0.1 fusion.39
  102.0 0.0 copy-done.2
  102.0 0.6 dynamic-slice.5
  103.2 8.0 %all-reduce = s32[64]{0:T(128)S(1)} all-reduce(s32[64]{0:T(128)S(1)} %fusion.39), channel_id=1, replica_groups=mesh['replica'=8,'tok'=4] {'replica'}, use_global_device_ids=true, to_apply=%add | all-reduce | flops 64 | bytes 512
  111.2 0.0 collective-permute-done
  111.3 5.8 %concatenate = bf16[114,4096]{1,0:T(8,128)(2,1)} concatenate(bf16[18,4096]{1,0:T(8,128)(2,1)S(1)} %collective-permute-done, bf16[96,4096]{1,0:T(8,128)(2,1)S(1)} %fusion), dimensions={0} | concatenate | bytes 1867776
  117.1 2.9 %bitcast_add_fusion = f32[90,4096]{1,0:T(8,128)S(1)} fusion(f32[1,90,4096]{2,0,1:T(1,128)} %param.11, bf16[114,4096]{1,0:T(8,128)(2,1)} %concatenate, u32[]{:S(6)} %subtract), kind=kLoop, calls=%fused_computation.4 | loop fusion | flops 1105920 | bytes 3686404 | tf_op jit(solution)/shard_map/add | solution.py:61
  119.9 0.6 gather_fusion
  120.5 0.1 gather.7
  120.6 0.4 fusion.7
  121.0 0.3 fusion.2
  121.3 0.1 reshape.90
  121.5 8.7 %all_gather.10 = bf16[64,1024]{1,0:T(8,128)(2,1)S(1)} all-gather(bf16[8,1024]{1,0:T(8,128)(2,1)S(1)} %reshape.90), channel_id=1, replica_groups=mesh['replica'=8,'tok'=4] {'replica'}, dimensions={0}, use_global_device_ids=true | all-gather | bytes 147456 | tf_op jit(solution)/shard_map/all_gather | solution.py:75
  130.2 0.3 fusion.11
  130.5 1.4 fusion.5
  131.9 3.9 %convolution_multiply_fusion = f32[90,64,64]{0,2,1:T(8,128)} fusion(f32[90,32,64]{0,2,1:T(8,128)S(1)} %fusion.5, f32[32]{0:T(128)S(1)} %compare_select_fusion.2, f32[64]{0:T(128)S(1)} %add_multiply_fusion), kind=kOutput, calls=%fused_computation.3 | convolution fusion | flops 141932544 | bytes 2212224 | tf_op jit(solution)/shard_map/ua,tuv,vb->tab/dot_general | solution.py:23
  135.8 2.8 %copy.26 = f32[90,4096]{1,0:T(8,128)} copy(f32[90,4096]{0,1:T(8,128)} %bitcast.61) | data formatting | bytes 2949120 | tf_op jit(solution)/shard_map/mul | solution.py:26
  138.6 2.6 %fusion.4 = bf16[1,90,4096]{2,1,0:T(8,128)(2,1)} fusion(f32[90,4096]{1,0:T(8,128)} %copy.26, bf16[90,4096]{1,0:T(8,128)(2,1)} %param.10), kind=kLoop, calls=%fused_computation.13 | loop fusion | flops 1105920 | bytes 2949120
  141.2 0.0 all-gather.3.cloned.1.call-update
  141.3 0.3 fusion.13
  141.6 0.6 convolution_negate_fusion
  142.2 0.1 reshape.106
  142.3 1.3 scatter_fusion
  143.7 2.6 %copy.30 = f32[1,90,4096]{2,0,1:T(1,128)} copy(f32[1,90,4096]{2,1,0:T(8,128)S(1)} %bitcast.60) | data formatting | bytes 2949120
  146.3 0.0 copy-start.1
  146.3 55.8 %all-gather.3.cloned.1.call-done = bf16[4,90,4096]{2,1,0:T(8,128)(2,1)} async-done(((bf16[1,90,4096]{2,1,0:T(8,128)(2,1)}), bf16[4,90,4096]{2,1,0:T(8,128)(2,1)}) %all-gather.3.cloned.1.call-update) | async-done | bytes 2949136 | tf_op jit(solution)/shard_map/all_gather | solution.py:83
  202.1 8.2 %reshape.92 = bf16[45,8,64,64]{3,2,1,0:T(8,128)(2,1)} reshape(bf16[4,90,4096]{2,1,0:T(8,128)(2,1)} %all-gather.3.cloned.1.call-done) | data formatting | bytes 5898240 | tf_op jit(solution)/shard_map/reshape | solution.py:36
  210.2 0.0 copy-done.1
  210.2 4.4 %fusion.1 = bf16[8,64,256]{2,1,0:T(8,128)(2,1)S(1)} fusion(bf16[45,8,64,64]{3,2,1,0:T(8,128)(2,1)} %reshape.92, bf16[256,45,64,1]{0,2,3,1:T(8,128)(2,1)S(1)} %bitcast.63), kind=kOutput, calls=%fused_computation.8 | convolution fusion | flops 755105792 | bytes 4685824 | tf_op jit(solution)/shard_map/tra,rcab->tcb/dot_general | solution.py:37
  214.7 0.8 copy.29
  (8 shorter events, 0.1 us)
Async XLA Ops:
  7.2 1.4 copy-start
  7.2 194.9 %all-gather.3.cloned.1.call-start = ((), (), s32[]{:S(2)}) async-start(), calls=%async_computation | async-start | bytes 3932160 | tf_op jit(solution)/shard_map/all_gather | solution.py:83
  36.2 63.7 %copy-start.3 = (s32[1,1,8]{2,1,0:T(1,128)S(1)}, s32[1,1,8]{2,1,0:T(1,128)}, u32[]{:S(2)}) copy-start(s32[1,1,8]{2,1,0:T(1,128)} %param.12) | copy-start | bytes 100
  36.2 64.4 %copy-start.4 = (u32[32]{0:T(128)S(1)}, u32[32]{0:T(128)}, u32[]{:S(2)}) copy-start(u32[32]{0:T(128)} %constant.48) | copy-start | bytes 388
  36.2 65.8 %copy-start.2 = (u32[32]{0:T(128)S(1)}, u32[32]{0:T(128)}, u32[]{:S(2)}) copy-start(u32[32]{0:T(128)} %constant.54) | copy-start | bytes 388
  98.2 13.1 %collective-permute-start = (bf16[18,4096]{1,0:T(8,128)(2,1)S(1)}, bf16[18,4096]{1,0:T(8,128)(2,1)S(1)}, u32[]{:S(2)}, u32[]{:S(2)}) collective-permute-start(bf16[18,4096]{1,0:T(8,128)(2,1)S(1)} %slice.2), channel_id=1, source_target_pairs={{0,1},{1,2},{2,3},{4,5},{5,6},{6,7},{8,9},{9,10},{10,11},{12,13},{... | collective-permute-start | bytes 442376
  146.3 64.0 %copy-start.1 = (bf16[256,2880]{0,1:T(8,128)(2,1)S(1)}, bf16[256,2880]{0,1:T(8,128)(2,1)}, u32[]{:S(2)}) copy-start(bf16[256,2880]{0,1:T(8,128)(2,1)} %param.9) | copy-start | bytes 4423684
Sparse Core Ops, SparseCore 0:
  141.4 60.6 all-gather.2
where the time goes:
time: 224 us; the launch traced here: 222 us
  blocking collectives  78.7 us (35%)
  waiting for transfers between devices  55.8 us (25%)
  local copies, waits for them, and re-layouts  47.9 us (21%)
  between operations  16.2 us (7%)
  matrix products  15.1 us (7%)
  other arithmetic  6.99 us (3%)
    unnamed x2, blocking collectives  69.9 us
    all_gather x1, waiting for transfers between devices, local(): new_full = lax.all_gather(new_part, 'tok', axis=0, tiled=True)  55.8 us
    convert_element_type x3, local copies, waits for them, and re-layouts, local(): tiled.astype(jnp.bfloat16)  24.1 us
    unnamed x17, local copies, waits for them, and re-layouts  11.9 us
    all_gather x1, blocking collectives, local(): lax.all_gather(flat_quads, 'replica', axis=0, tiled=True)  8.73 us
    reshape x1, local copies, waits for them, and re-layouts, forward(): matrix = new_tiles.reshape(row_tiles, col_tiles, TILE, TILE)  8.17 us
    dot_general x2, matrix products, rebuild(): jnp.einsum('ua,tuv,vb->tab', keep_rows, quads, keep_rows, precision=lax.P...  5.25 us
  transfers between devices with their start and end apart: 2, of which 1 were waited for; matrix products, arithmetic and copies ran while one was open for 3% of the time, Pallas kernels for 0%

commit v1 on v0

--- a/solution.py
+++ b/solution.py
@@ -8,6 +8,24 @@
 KEEP = 32
 momentum_decay = 0.9
 step_size = 0.01
+
+
+def laid_out(tiles, dim):
+    tiles = jnp.moveaxis(tiles, 0, dim)
+    dims = tiles.shape
+    return tiles.reshape(*dims[:dim], dims[dim] * dims[dim + 1], *dims[dim + 2 :])
+
+
+def doubled(x, axis):
+    count = lax.axis_size(axis)
+    pieces = x[None]
+    for level in range(count.bit_length() - 1):
+        stride = 1 << level
+        other = lax.ppermute(pieces, axis, [(i, i ^ stride) for i in range(count)])
+        both = jnp.stack([pieces, other])
+        upper = lax.axis_index(axis) >> level & 1
+        pieces = jnp.where(upper == 0, both, both[::-1]).reshape(-1, *x.shape)
+    return pieces
 
 
 def cosine_rows(count):
@@ -80,7 +98,7 @@
         one_hot, all_quads, (((0,), (0,)), ((), ())), preferred_element_type=jnp.float32
     )
     new_part = rebuild(summed, weight_tiles, keep_rows)
-    new_full = lax.all_gather(new_part, "tok", axis=0, tiled=True)
+    new_full = laid_out(doubled(new_part, "tok"), 0)
     values = forward(next_inputs, new_full)
     return (values, new_momentum[None])
 

time: 224 us -> 247 us (1.10)
  waiting for transfers between devices: 55.8 us -> 80.5 us
  between operations: 16.2 us -> 2.78 us
  other arithmetic: 6.99 us -> 13.5 us
  local copies, waits for them, and re-layouts: 47.9 us -> 53 us
    ppermute x0 -> x2, waiting for transfers between devices: none -> 80.5 us  [doubled(): other = lax.ppermute(pieces, axis, [(i, i ^ stride) for i in range(count)])]
    all_gather x1 -> x0, waiting for transfers between devices: 55.8 us -> none  [local(): new_full = lax.all_gather(new_part, 'tok', axis=0, tiled=True)]
    another operation x0 -> x1, local copies, waits for them, and re-layouts: none -> 8.29 us  [forward(): matrix = new_tiles.reshape(row_tiles, col_tiles, TILE, TILE)]
    another operation x0 -> x4, other arithmetic: none -> 6.39 us  [doubled(): both = jnp.stack([pieces, other])]
    reshape x1, local copies, waits for them, and re-layouts: 8.17 us -> 2.65 us  [doubled(): pieces = jnp.where(upper == 0, both, both[::-1]).reshape(-1, *x.shape)]
    unnamed x2 -> x1, other arithmetic: 2.74 us -> 0.1 us
    select_n x0 -> x1, other arithmetic: none -> 2.5 us  [doubled(): pieces = jnp.where(upper == 0, both, both[::-1]).reshape(-1, *x.shape)]
    unnamed x17 -> x19, local copies, waits for them, and re-layouts: 11.9 us -> 11.9 us
  transfers between devices with their start and end apart: 2 -> 3, of which waited for: 1 -> 2; matrix products, arithmetic and copies ran while one was open for 3% -> 3% of each run, Pallas kernels for 0% -> 0%
where the time goes in v1:
time: 247 us; the launch traced here: 246 us
  waiting for transfers between devices  80.5 us (33%)
  blocking collectives  78.7 us (32%)
  local copies, waits for them, and re-layouts  53 us (21%)
  matrix products  15.1 us (6%)
  other arithmetic  13.5 us (5%)
  between operations  2.78 us (1%)
    ppermute x2, waiting for transfers between devices, doubled(): other = lax.ppermute(pieces, axis, [(i, i ^ stride) for i in range(count)])  80.5 us
    unnamed x2, blocking collectives  69.9 us
    convert_element_type x3, local copies, waits for them, and re-layouts, local(): tiled.astype(jnp.bfloat16)  24.1 us
    unnamed x19, local copies, waits for them, and re-layouts  11.9 us
    all_gather x1, blocking collectives, local(): lax.all_gather(flat_quads, 'replica', axis=0, tiled=True)  8.73 us
    another operation x1, local copies, waits for them, and re-layouts, forward(): matrix = new_tiles.reshape(row_tiles, col_tiles, TILE, TILE)  8.29 us
    another operation x4, other arithmetic, doubled(): both = jnp.stack([pieces, other])  6.39 us
    dot_general x2, matrix products, rebuild(): jnp.einsum('ua,tuv,vb->tab', keep_rows, quads, keep_rows, precision=lax.P...  5.24 us
  transfers between devices with their start and end apart: 3, of which 2 were waited for; matrix products, arithmetic and copies ran while one was open for 3% of the time, Pallas kernels for 0%

profile of v1, /device:TPU:0, one launch (start us, length us, event | category | flops | bytes accessed | tf_op | source)
XLA Modules:
  0.0 245.8 jit_solution(10565418690630978139)
XLA Ops:
  0.6 0.0 copy-start
  0.6 1.4 copy-done
  2.0 3.5 %multiply_convert_fusion = bf16[2880,512]{1,0:T(8,128)(2,1)} fusion(bf16[256,2880]{0,1:T(8,128)(2,1)S(1)} %copy-done, bf16[256,512]{1,0:T(8,128)(2,1)} %param.8), kind=kOutput, calls=%fused_computation.2 | convolution fusion | flops 757923840 | bytes 4685824 | tf_op jit(solution)/shard_map/dot_general | solution.py:69
  5.5 8.4 %convert_element_type.37 = bf16[45,64,8,64]{3,2,1,0:T(8,128)(2,1)} reshape(bf16[2880,512]{1,0:T(8,128)(2,1)} %multiply_convert_fusion) | data formatting | bytes 5898240 | tf_op jit(solution)/shard_map/convert_element_type | solution.py:77
  13.9 7.0 %copy.35 = bf16[45,8,64,64]{3,2,1,0:T(8,128)(2,1)} copy(bf16[45,8,64,64]{3,1,2,0:T(8,128)(2,1)} %bitcast.69) | data formatting | bytes 5898240 | tf_op jit(solution)/shard_map/convert_element_type | solution.py:77
  20.9 8.7 %convert_element_type.39 = bf16[360,4096]{1,0:T(8,128)(2,1)} reshape(bf16[45,8,64,64]{3,2,1,0:T(8,128)(2,1)} %copy.35) | data formatting | bytes 5898240 | tf_op jit(solution)/shard_map/convert_element_type | solution.py:77
  29.7 61.9 %fusion = bf16[96,4096]{1,0:T(8,128)(2,1)S(1)} fusion(bf16[360,4096]{1,0:T(8,128)(2,1)} %convert_element_type.39), kind=kCustom, calls=%all-reduce-scatter | all-reduce-scatter fusion | flops 1572865 | bytes 3736064
  91.6 1.7 collective-permute-start.2
  93.3 0.0 copy-done.4
  94.1 0.0 copy-done.5
  94.1 0.6 dynamic-slice
  95.3 0.1 fusion.40
  95.4 0.0 copy-done.3
  95.4 0.6 dynamic-slice.5
  96.7 8.0 %all-reduce = s32[64]{0:T(128)S(1)} all-reduce(s32[64]{0:T(128)S(1)} %fusion.40), channel_id=1, replica_groups=mesh['replica'=8,'tok'=4] {'replica'}, use_global_device_ids=true, to_apply=%add | all-reduce | flops 64 | bytes 512
  104.7 0.0 collective-permute-done.2
  104.7 5.8 %concatenate = bf16[114,4096]{1,0:T(8,128)(2,1)} concatenate(bf16[18,4096]{1,0:T(8,128)(2,1)S(1)} %collective-permute-done.2, bf16[96,4096]{1,0:T(8,128)(2,1)S(1)} %fusion), dimensions={0} | concatenate | bytes 1867776
  110.5 2.9 %bitcast_add_fusion = f32[90,4096]{1,0:T(8,128)S(1)} fusion(f32[1,90,4096]{2,0,1:T(1,128)} %param.11, bf16[114,4096]{1,0:T(8,128)(2,1)} %concatenate, u32[]{:S(6)} %subtract), kind=kLoop, calls=%fused_computation.8 | loop fusion | flops 1105920 | bytes 3686404 | tf_op jit(solution)/shard_map/add | solution.py:79
  113.4 0.6 gather_fusion
  114.0 0.1 gather.7
  114.1 0.4 fusion.8
  114.5 0.3 fusion.4
  114.8 0.1 reshape.90
  114.9 8.7 %all_gather.7 = bf16[64,1024]{1,0:T(8,128)(2,1)S(1)} all-gather(bf16[8,1024]{1,0:T(8,128)(2,1)S(1)} %reshape.90), channel_id=1, replica_groups=mesh['replica'=8,'tok'=4] {'replica'}, dimensions={0}, use_global_device_ids=true | all-gather | bytes 147456 | tf_op jit(solution)/shard_map/all_gather | solution.py:93
  123.7 0.3 fusion.12
  124.0 1.4 fusion.6
  125.3 3.9 %convolution_multiply_fusion = f32[90,64,64]{0,2,1:T(8,128)} fusion(f32[90,32,64]{0,2,1:T(8,128)S(1)} %fusion.6, f32[32]{0:T(128)S(1)} %compare_select_fusion.2, f32[64]{0:T(128)S(1)} %add_multiply_fusion), kind=kOutput, calls=%fused_computation.6 | convolution fusion | flops 141932544 | bytes 2212224 | tf_op jit(solution)/shard_map/ua,tuv,vb->tab/dot_general | solution.py:41
  129.2 2.9 %copy.39 = f32[90,4096]{1,0:T(8,128)} copy(f32[90,4096]{0,1:T(8,128)} %bitcast.71) | data formatting | bytes 2949120 | tf_op jit(solution)/shard_map/mul | solution.py:44
  132.1 3.0 %fusion.49 = (bf16[1,1,90,4096]{3,2,1,0:T(8,128)(2,1)}, bf16[1,90,4096]{2,1,0:T(8,128)(2,1)}) fusion(f32[90,4096]{1,0:T(8,128)} %copy.39, bf16[90,4096]{1,0:T(8,128)(2,1)} %param.10), kind=kLoop, calls=%fused_computation.73 | loop fusion | flops 1105920 | bytes 3686400 | tf_op jit(solution)/shard_map/stack;broadcast_in_dim | solution.py:25
  135.1 0.3 collective-permute-start
  135.4 19.8 %collective-permute-done = bf16[1,90,4096]{2,1,0:T(8,128)(2,1)} collective-permute-done((bf16[1,90,4096]{2,1,0:T(8,128)(2,1)}, bf16[1,90,4096]{2,1,0:T(8,128)(2,1)}, u32[]{:S(2)}, u32[]{:S(2)}) %collective-permute-start) | collective-permute-done | bytes 737312 | tf_op jit(solution)/shard_map/ppermute | solution.py:24
  155.2 1.5 pad_maximum_fusion.1
  156.7 1.6 fusion.3
  158.3 2.7 %copy.40 = bf16[2,90,4096]{2,0,1:T(2,128)(2,1)} copy(bf16[2,90,4096]{2,1,0:T(8,128)(2,1)S(1)} %get-tuple-element.13) | data formatting | bytes 2949120 | tf_op jit(solution)/shard_map/reshape | solution.py:27
  160.9 0.3 collective-permute-start.1
  161.3 0.3 fusion.14
  161.6 0.6 convolution_negate_fusion
  162.2 0.1 reshape.106
  162.3 1.6 scatter_fusion
  163.9 2.6 %copy.45 = f32[1,90,4096]{2,0,1:T(1,128)} copy(f32[1,90,4096]{2,1,0:T(8,128)S(1)} %bitcast.70) | data formatting | bytes 2949120
  166.5 60.7 %collective-permute-done.1 = bf16[2,90,4096]{2,0,1:T(2,128)(2,1)} collective-permute-done((bf16[2,90,4096]{2,0,1:T(2,128)(2,1)}, bf16[2,90,4096]{2,0,1:T(2,128)(2,1)}, u32[]{:S(2)}, u32[]{:S(2)}) %collective-permute-start.1) | collective-permute-done | bytes 1474592 | tf_op jit(solution)/shard_map/ppermute | solution.py:24
  227.2 2.2 copy.58
  229.5 0.0 copy-done.1
  229.5 0.3 pad_maximum_fusion
  229.8 2.5 %reverse_select_fusion = bf16[2,2,90,4096]{3,2,1,0:T(8,128)(2,1)} fusion(bf16[2,2,90,4096]{3,2,1,0:T(8,128)(2,1)S(1)} %pad_maximum_fusion, pred[]{:T(512)S(6)} %eq.40), kind=kLoop, calls=%fused_computation.3 | loop fusion | flops 1474560 | bytes 5898241 | tf_op jit(solution)/shard_map/jit(_where)/select_n | solution.py:27
  232.3 8.3 %reshape_reshape_reshape.3 = bf16[45,8,64,64]{3,2,1,0:T(8,128)(2,1)} reshape(bf16[2,2,90,4096]{3,2,1,0:T(8,128)(2,1)} %reverse_select_fusion) | data formatting | bytes 5898240 | tf_op jit(solution)/shard_map/reshape;reshape;reshape | solution.py:54
  240.6 4.4 %fusion.1 = bf16[8,64,256]{2,1,0:T(8,128)(2,1)S(1)} fusion(bf16[45,8,64,64]{3,2,1,0:T(8,128)(2,1)} %reshape_reshape_reshape.3, bf16[256,45,64,1]{0,2,3,1:T(8,128)(2,1)S(1)} %bitcast.74), kind=kOutput, calls=%fused_computation.13 | convolution fusion | flops 755105792 | bytes 4685824 | tf_op jit(solution)/shard_map/tra,rcab->tcb/dot_general | solution.py:55
  245.0 0.8 copy.44
  (14 shorter events, 0.1 us)
Async XLA Ops:
  0.6 1.4 copy-start
  29.7 63.7 %copy-start.4 = (s32[1,1,8]{2,1,0:T(1,128)S(1)}, s32[1,1,8]{2,1,0:T(1,128)}, u32[]{:S(2)}) copy-start(s32[1,1,8]{2,1,0:T(1,128)} %param.12) | copy-start | bytes 100
  29.7 64.4 %copy-start.5 = (u32[32]{0:T(128)S(1)}, u32[32]{0:T(128)}, u32[]{:S(2)}) copy-start(u32[32]{0:T(128)} %constant.55) | copy-start | bytes 388
  29.7 65.8 %copy-start.3 = (u32[32]{0:T(128)S(1)}, u32[32]{0:T(128)}, u32[]{:S(2)}) copy-start(u32[32]{0:T(128)} %constant.61) | copy-start | bytes 388
  91.6 13.1 %collective-permute-start.2 = (bf16[18,4096]{1,0:T(8,128)(2,1)S(1)}, bf16[18,4096]{1,0:T(8,128)(2,1)S(1)}, u32[]{:S(2)}, u32[]{:S(2)}) collective-permute-start(bf16[18,4096]{1,0:T(8,128)(2,1)S(1)} %slice.2), channel_id=1, source_target_pairs={{0,1},{1,2},{2,3},{4,5},{5,6},{6,7},{8,9},{9,10},{10,11},{12,13},{... | collective-permute-start | bytes 442376
  135.1 20.1 %collective-permute-start = (bf16[1,90,4096]{2,1,0:T(8,128)(2,1)}, bf16[1,90,4096]{2,1,0:T(8,128)(2,1)}, u32[]{:S(2)}, u32[]{:S(2)}) collective-permute-start(bf16[1,90,4096]{2,1,0:T(8,128)(2,1)} %get-tuple-element.11), channel_id=1, source_target_pairs={{0,1},{1,0},{2,3},{3,2},{4,5},{5,4},{6,7},{7,6},{8,9},{9,8},{10,11... | collective-permute-start | bytes 2211848 | tf_op jit(solution)/shard_map/ppermute | solution.py:24
  160.9 66.3 %collective-permute-start.1 = (bf16[2,90,4096]{2,0,1:T(2,128)(2,1)}, bf16[2,90,4096]{2,0,1:T(2,128)(2,1)}, u32[]{:S(2)}, u32[]{:S(2)}) collective-permute-start(bf16[2,90,4096]{2,0,1:T(2,128)(2,1)} %copy.40), channel_id=1, source_target_pairs={{0,2},{1,3},{2,0},{3,1},{4,6},{5,7},{6,4},{7,5},{8,10},{9,11},{10,... | collective-permute-start | bytes 4423688 | tf_op jit(solution)/shard_map/ppermute | solution.py:24
  166.5 62.9 %copy-start.1 = (bf16[1,2,90,4096]{3,2,1,0:T(8,128)(2,1)S(1)}, bf16[1,2,90,4096]{3,2,1,0:T(8,128)(2,1)}, u32[]{:S(2)}) copy-start(bf16[1,2,90,4096]{3,2,1,0:T(8,128)(2,1)} %get-tuple-element.12) | copy-start | bytes 4423684
  232.3 8.3 %copy-start.2 = (bf16[256,2880]{0,1:T(8,128)(2,1)S(1)}, bf16[256,2880]{0,1:T(8,128)(2,1)}, u32[]{:S(2)}) copy-start(bf16[256,2880]{0,1:T(8,128)(2,1)} %param.9) | copy-start | bytes 4423684
